TPU v7x, 32 devices: a whole 2x2x4 slice. The times are simulated.
32 devices in a mesh: seq: 8 (over y, x, core), head: 4 (over z).
Axes of the slice: x: 2, y: 2, z: 4, core: 2. Of those that a mesh axis runs over, the one named last changes fastest.
Arguments:
- inputs: bfloat16 [4096, 4096], P('seq'), may hold values from -6 to 6
- queries: bfloat16 [4096, 4096], P('seq', 'head'), may hold values from -6 to 6
- keys: bfloat16 [4096, 4096], P('seq', 'head'), may hold values from -6 to 6
- values: bfloat16 [4096, 4096], P('seq', 'head'), may hold values from -6 to 6
- out_grad: bfloat16 [4096, 4096], P('seq', 'head'), may hold values from -6 to 6
- value_weight: bfloat16 [4096, 4096], P('seq', 'head'), may hold values from -0.125 to 0.125
Outputs:
- grad_input: bfloat16 [4096, 4096], P('seq', 'head')
- grad_query: bfloat16 [4096, 4096], P('seq', 'head')
- grad_key: bfloat16 [4096, 4096], P('seq', 'head')
- grad_value: bfloat16 [4096, 4096], P('seq', 'head')
- grad_weight: float32 [4096, 4096], P('seq', 'head')
All inputs are finite; a program needn't handle non-finite values.
Results may differ from a plain program's by a relative error of at most 0.015.
Values may be sent and summed in bfloat16 or wider, within the bound.
A program may use at most 128 MiB of HBM per device.

v0:
```python
import math
import jax
import jax.numpy as jnp
from jax import lax
from jax.sharding import PartitionSpec as P

HEAD_DIM = 128


def carried_in(shard, axis, combine, identity, reverse):
    count, here = (lax.axis_size(axis), lax.axis_index(axis))
    everything = lax.all_gather(shard.astype(jnp.bfloat16), axis)
    start = jnp.broadcast_to(jnp.asarray(identity, shard.dtype), shard.shape)

    def lap(k, before):
        at = count - 1 - k if reverse else k
        reached = at > here if reverse else at < here
        new = combine(before, everything[at].astype(shard.dtype))
        return jnp.where(reached, new, before)

    return lax.fori_loop(0, count, lap, start)


def add_states(earlier, later):
    return earlier + later


def local(inputs, queries, keys, values, out_grad, value_weight):
    f32 = jnp.float32
    high = lax.Precision.HIGHEST
    rows = queries.shape[0]
    width = queries.shape[1]
    nheads = width // HEAD_DIM
    first = lax.axis_index("seq") * rows
    posit = (first + jnp.arange(rows, dtype=jnp.int32)).astype(f32)
    factor = 1.0 / jnp.sqrt(HEAD_DIM * (posit + 1.0))
    q3 = queries.reshape(rows, nheads, HEAD_DIM)
    k3 = keys.reshape(rows, nheads, HEAD_DIM)
    v3 = values.reshape(rows, nheads, HEAD_DIM)
    o3 = out_grad.reshape(rows, nheads, HEAD_DIM)
    o3wide = o3.astype(f32)
    state_kv = jnp.einsum("thi,thj->hij", k3, v3, preferred_element_type=f32)
    state_qo = jnp.einsum(
        "thi,thj->hij", q3.astype(f32), o3wide * factor[:, None, None], precision=high
    )
    empty_state = jnp.zeros_like(state_kv)
    prefix = carried_in(state_kv, "seq", add_states, empty_state, False)
    suffix = carried_in(state_qo, "seq", add_states, empty_state, True)
    index = jnp.arange(rows, dtype=jnp.int32)
    lower = (index[:, None] >= index[None, :])[None]
    score_qk = (
        jnp.einsum("thd,shd->hts", q3, k3, preferred_element_type=f32) * factor[None, :, None]
    )
    score_qk = jnp.where(lower, score_qk, 0.0).astype(jnp.bfloat16)
    score_ov = (
        jnp.einsum("thd,shd->hts", o3, v3, preferred_element_type=f32) * factor[None, :, None]
    )
    score_ov = jnp.where(lower, score_ov, 0.0).astype(jnp.bfloat16)
    dq = jnp.einsum("hts,shd->thd", score_ov, k3, preferred_element_type=f32)
    dq = dq + factor[:, None, None] * jnp.einsum("thj,hij->thi", o3wide, prefix, precision=high)
    dk = jnp.einsum("hts,thd->shd", score_ov, q3, preferred_element_type=f32)
    dk = dk + jnp.einsum("shj,hij->shi", v3.astype(f32), suffix, precision=high)
    dv = jnp.einsum("hts,thd->shd", score_qk, o3, preferred_element_type=f32)
    dv = dv + jnp.einsum("shi,hij->shj", k3.astype(f32), suffix, precision=high)
    grad_query = dq.reshape(rows, width).astype(jnp.bfloat16)
    grad_key = dk.reshape(rows, width).astype(jnp.bfloat16)
    grad_value = dv.reshape(rows, width).astype(jnp.bfloat16)
    both_last = (((1,), (1,)), ((), ()))
    partial_grad = lax.dot_general(
        grad_value,
        lax.all_gather(value_weight, "seq", axis=0, tiled=True),
        both_last,
        preferred_element_type=f32,
    )
    grad_input = lax.psum_scatter(
        partial_grad.astype(jnp.bfloat16), "head", scatter_dimension=1, tiled=True
    )
    wscale = 1.0 / math.sqrt(rows * lax.axis_size("seq"))
    product = lax.dot_general(
        inputs, grad_value, (((0,), (0,)), ((), ())), preferred_element_type=f32
    )
    grad_weight = lax.psum_scatter(
        (product * wscale).astype(jnp.bfloat16), "seq", scatter_dimension=0, tiled=True
    ).astype(jnp.float32)
    return (grad_input, grad_query, grad_key, grad_value, grad_weight)


def solution(mesh):
    in_specs = (
        P("seq", None),
        P("seq", "head"),
        P("seq", "head"),
        P("seq", "head"),
        P("seq", "head"),
        P("seq", "head"),
    )
    out_specs = (
        P("seq", "head"),
        P("seq", "head"),
        P("seq", "head"),
        P("seq", "head"),
        P("seq", "head"),
    )
    return jax.shard_map(local, mesh=mesh, in_specs=in_specs, out_specs=out_specs, check_vma=False)
```

profile of v0, /device:TPU:0, one launch (start us, length us, event | category | flops | bytes accessed | tf_op | source)
XLA Modules:
  0.0 291.6 jit_solution(2182478048408645564)
XLA Ops:
  7.2 0.0 copy-start
  7.2 0.0 all-gather.8.cloned.1.call-start
  7.2 2.4 copy.48
  9.6 1.5 copy.49
  11.1 2.4 fusion.16
  13.5 0.8 copy.32
  14.4 0.0 all-gather.8.cloned.1.call-update
  14.4 0.0 all-gather.6.cloned.1.call-start
  14.4 0.7 all-gather.6.cloned.1.call-update
  15.1 0.0 all-gather.10.cloned.1.call-start
  15.2 0.0 copy-done
  15.2 2.4 convolution_convert_fusion.1
  17.6 0.0 all-gather.10.cloned.1.call-update
  17.7 0.0 reduce-scatter.5.cloned.1.call-start
  17.7 0.1 iota_compare_fusion
  17.8 5.0 %fusion.1 = f32[8,512,128]{1,2,0:T(8,128)} fusion(bf16[512,8,128]{0,2,1:T(8,128)(2,1)} %bitcast.99, f32[512]{0:T(512)S(1)} %multiply_rsqrt_fusion, pred[512,512]{1,0:T(8,128)(4,1)S(1)} %iota_compare_fusion, bf16[512,8,128]{0,2,1:T(8,128)(2,1)S(1)} %bitcast.96, bf16[512,1024]{1,0:T(8,128)(2,1)} %param.12), kind=kOutput, calls=%fused_computation.7 | convolution fusion | flops 1080033280 | bytes 5507072 | tf_op jit(solution)/shard_map/hts,thd->shd/dot_general | solution.py:63
  22.8 22.2 %all-gather.8.cloned.1.call-done = bf16[64,128,128]{2,1,0:T(8,128)(2,1)} async-done(((bf16[8,128,128]{2,1,0:T(8,128)(2,1)}), bf16[64,128,128]{2,1,0:T(8,128)(2,1)}) %all-gather.8.cloned.1.call-update) | async-done | bytes 2097168 | tf_op jit(solution)/shard_map/all_gather | solution.py:12
  45.0 10.1 %while.30 = (s32[]{:T(128)}, f32[8,128,128]{2,1,0:T(8,128)S(1)}, s32[]{:T(128)}, bf16[8,8,128,128]{3,2,1,0:T(8,128)(2,1)}, s32[]{:T(128)}, /*index=5*/s32[]{:T(128)}, s32[]{:T(128)}, s32[]{:T(128)}) while((s32[]{:T(128)}, f32[8,128,128]{2,1,0:T(8,128)S(1)}, s32[]{:T(128)}, bf16[8,8,128,128]{3,2,1,0:T(8,128)(2,1)}, s32[]{:T(128)}, ...), condition=%wide.region_1.2_spmd.clone, body=%wide.region_0.1_spmd.clone.sunk | while | flops 524296 | bytes 1310883 | solution.py:21
  45.0 1.2 add_select_fusion.4
  46.3 1.2 add_select_fusion.4
  47.6 1.2 add_select_fusion.4
  48.8 1.2 add_select_fusion.4
  50.1 1.2 add_select_fusion.4
  51.3 1.2 add_select_fusion.4
  52.6 1.3 add_select_fusion.4
  53.9 1.3 add_select_fusion.4
  55.2 0.0 copy-start.4
  55.2 3.4 %fusion.9 = bf16[512,8,128]{0,2,1:T(8,128)(2,1)S(1)} fusion(f32[8,512,128]{1,2,0:T(8,128)} %fusion.1, f32[8,128,128]{2,1,0:T(8,128)S(1)} %get-tuple-element.194, bf16[512,1024]{1,0:T(8,128)(2,1)} %param.12), kind=kOutput, calls=%fused_computation.17 | convolution fusion | flops 806354944 | bytes 4718592 | tf_op jit(solution)/shard_map/shi,hij->shj/dot_general | solution.py:64
  58.6 0.0 copy-start.3
  58.6 1.0 copy-done.3
  59.6 0.0 copy-done.4
  59.6 6.8 %fusion = bf16[4096,1024]{0,1:T(8,128)(2,1)} fusion(bf16[512,1024]{0,1:T(8,128)(2,1)S(1)} %bitcast.102, bf16[512,4096]{1,0:T(8,128)(2,1)S(1)} %copy-done.4), kind=kOutput, calls=%fused_computation.5 | convolution fusion | flops 4303355904 | bytes 13631488 | tf_op jit(solution)/shard_map/dot_general | solution.py:79
  66.4 0.0 reduce-scatter.5.cloned.1.call-update
  66.4 0.2 reduce-scatter.3.cloned.1.call-start
  66.6 34.6 %all-gather.6.cloned.1.call-done = bf16[4096,1024]{1,0:T(8,128)(2,1)} async-done(((bf16[512,1024]{1,0:T(8,128)(2,1)}), bf16[4096,1024]{1,0:T(8,128)(2,1)}) %all-gather.6.cloned.1.call-update) | async-done | bytes 8388624 | tf_op jit(solution)/shard_map/all_gather | solution.py:71
  101.2 10.2 %convolution_convert_fusion = bf16[512,4096]{1,0:T(8,128)(2,1)} fusion(bf16[512,1024]{0,1:T(8,128)(2,1)} %bitcast.103, bf16[4096,1024]{1,0:T(8,128)(2,1)} %all-gather.6.cloned.1.call-done), kind=kOutput, calls=%fused_computation.6 | convolution fusion | flops 4297064448 | bytes 13631488 | tf_op jit(solution)/shard_map/dot_general | solution.py:69
  111.5 0.0 reduce-scatter.3.cloned.1.call-update
  111.5 0.0 copy-start.2
  111.5 3.1 %select_convert_fusion = bf16[8,512,512]{2,1,0:T(8,128)(2,1)S(1)} fusion(f32[512]{0:T(512)S(1)} %multiply_rsqrt_fusion, pred[512,512]{1,0:T(8,128)(4,1)S(1)} %iota_compare_fusion, bf16[512,8,128]{0,2,1:T(8,128)(2,1)} %bitcast.100, bf16[512,1024]{1,0:T(8,128)(2,1)S(1)} %copy-done), kind=kOutput, calls=%fused_computation.3 | convolution fusion | flops 543162368 | bytes 6555648 | tf_op jit(solution)/shard_map/thd,shd->hts/dot_general | solution.py:56
  114.6 0.0 copy-done.2
  114.6 2.8 fusion.24
  117.4 2.1 fusion.38
  119.5 0.0 copy-start.1
  119.5 2.4 copy.45
  121.9 9.1 %all-gather.10.cloned.1.call-done = bf16[64,128,128]{2,1,0:T(8,128)(2,1)} async-done(((bf16[8,128,128]{2,1,0:T(8,128)(2,1)}), bf16[64,128,128]{2,1,0:T(8,128)(2,1)}) %all-gather.10.cloned.1.call-update) | async-done | bytes 2097168 | tf_op jit(solution)/shard_map/all_gather | solution.py:12
  130.9 10.0 %while.31 = (s32[]{:T(128)}, f32[8,128,128]{2,1,0:T(8,128)S(1)}, s32[]{:T(128)}, bf16[8,8,128,128]{3,2,1,0:T(8,128)(2,1)}, s32[]{:T(128)}, /*index=5*/s32[]{:T(128)}) while((s32[]{:T(128)}, f32[8,128,128]{2,1,0:T(8,128)S(1)}, s32[]{:T(128)}, bf16[8,8,128,128]{3,2,1,0:T(8,128)(2,1)}, s32[]{:T(128)}, /*index=5*/s32[]{:T(128)}) %tuple.90), condition=%wide.region_4.5_spmd.clone, body=%wide.region_3.4_spmd.clone.sunk | while | flops 524292 | bytes 1310821 | solution.py:21
  130.9 1.2 add_select_fusion.5
  132.2 1.2 add_select_fusion.5
  133.4 1.2 add_select_fusion.5
  134.7 1.2 add_select_fusion.5
  135.9 1.2 add_select_fusion.5
  137.2 1.2 add_select_fusion.5
  138.5 1.2 add_select_fusion.5
  139.7 1.2 add_select_fusion.5
  141.0 0.0 copy-done.1
  141.0 4.0 %fusion.8 = bf16[512,8,128]{0,2,1:T(8,128)(2,1)} fusion(f32[8,512,128]{1,2,0:T(8,128)} %fusion.24, f32[8,128,128]{2,1,0:T(8,128)S(1)} %get-tuple-element.195, bf16[512,8,128]{0,2,1:T(8,128)(2,1)S(1)} %bitcast.101, f32[512]{0:T(512)S(1)} %multiply_rsqrt_fusion), kind=kOutput, calls=%fused_computation.15 | convolution fusion | flops 806879232 | bytes 4720640 | tf_op jit(solution)/shard_map/thj,hij->thi/dot_general | solution.py:60
  145.0 2.4 copy.43
  147.5 3.0 %fusion.7 = bf16[512,8,128]{0,2,1:T(8,128)(2,1)S(1)} fusion(f32[8,512,128]{1,2,0:T(8,128)} %fusion.38, f32[8,128,128]{2,1,0:T(8,128)S(1)} %get-tuple-element.194, bf16[512,1024]{1,0:T(8,128)(2,1)S(1)} %copy-done), kind=kOutput, calls=%fused_computation.13 | convolution fusion | flops 806354944 | bytes 4718592 | tf_op jit(solution)/shard_map/shj,hij->shi/dot_general | solution.py:62
  150.4 1.3 copy.44
  151.8 53.8 %reduce-scatter.5.cloned.1.call-done = bf16[512,1024]{0,1:T(8,128)(2,1)} async-done(((bf16[4096,1024]{0,1:T(8,128)(2,1)}), bf16[512,1024]{0,1:T(8,128)(2,1)}) %reduce-scatter.5.cloned.1.call-update) | async-done | bytes 1048592 | tf_op jit(solution)/shard_map/reduce_scatter | solution.py:82
  205.6 2.6 copy.46
  208.1 77.0 %reduce-scatter.3.cloned.1.call-done = bf16[512,1024]{1,0:T(8,128)(2,1)} async-done(((bf16[512,4096]{1,0:T(8,128)(2,1)}), bf16[512,1024]{1,0:T(8,128)(2,1)}) %reduce-scatter.3.cloned.1.call-update) | async-done | bytes 1048592 | tf_op jit(solution)/shard_map/reduce_scatter | solution.py:75
  (3 shorter events, 0.0 us)
Async XLA Ops:
  7.2 8.0 %copy-start = (bf16[512,1024]{1,0:T(8,128)(2,1)S(1)}, bf16[512,1024]{1,0:T(8,128)(2,1)}, u32[]{:S(2)}) copy-start(bf16[512,1024]{1,0:T(8,128)(2,1)} %param.13) | copy-start | bytes 3145732
  7.2 37.9 %all-gather.8.cloned.1.call-start = ((), (), s32[]{:S(2)}) async-start(), calls=%async_computation.5 | async-start | bytes 2359296 | tf_op jit(solution)/shard_map/all_gather | solution.py:12
  14.4 86.8 %all-gather.6.cloned.1.call-start = ((), (), s32[]{:S(2)}) async-start(), calls=%async_computation.2 | async-start | bytes 9437184 | tf_op jit(solution)/shard_map/all_gather | solution.py:71
  15.1 115.8 %all-gather.10.cloned.1.call-start = ((), (), s32[]{:S(2)}) async-start(), calls=%async_computation.6 | async-start | bytes 2359296 | tf_op jit(solution)/shard_map/all_gather | solution.py:12
  17.7 187.9 %reduce-scatter.5.cloned.1.call-start = ((), (), s32[]{:S(2)}) async-start(), calls=%async_computation.4 | async-start | bytes 9437184 | tf_op jit(solution)/shard_map/reduce_scatter | solution.py:82
  55.2 4.4 %copy-start.4 = (bf16[512,4096]{1,0:T(8,128)(2,1)S(1)}, bf16[512,4096]{1,0:T(8,128)(2,1)}, u32[]{:S(2)}) copy-start(bf16[512,4096]{1,0:T(8,128)(2,1)} %param.10) | copy-start | bytes 12582916
  58.6 1.0 copy-start.3
  66.4 218.7 %reduce-scatter.3.cloned.1.call-start = ((), (), s32[]{:S(2)}) async-start(), calls=%async_computation.3 | async-start | bytes 5242880 | tf_op jit(solution)/shard_map/reduce_scatter | solution.py:75
  111.5 3.1 %copy-start.2 = (bf16[512,1024]{1,0:T(8,128)(2,1)S(1)}, bf16[512,1024]{1,0:T(8,128)(2,1)}, u32[]{:S(2)}) copy-start(bf16[512,1024]{1,0:T(8,128)(2,1)} %param.12) | copy-start | bytes 3145732
  119.5 21.5 %copy-start.1 = (bf16[512,1024]{0,1:T(8,128)(2,1)S(1)}, bf16[512,1024]{0,1:T(8,128)(2,1)}, u32[]{:S(2)}) copy-start(bf16[512,1024]{0,1:T(8,128)(2,1)} %copy.48) | copy-start | bytes 3145732
Sparse Core Ops, SparseCore 0:
  14.5 30.4 all-gather.7
  46.9 54.2 all-gather.5
  103.1 27.7 all-gather.9
  134.2 71.2 reduce-scatter.4
  208.3 76.7 reduce-scatter.2
where the time goes:
time: 293 us; the launch traced here: 292 us
  waiting for transfers between devices  197 us (67%)
  matrix products  45.3 us (15%)
  other arithmetic  19.9 us (7%)
  local copies, waits for them, and re-layouts  14.3 us (5%)
  between operations  13.9 us (5%)
    reduce_scatter x1, waiting for transfers between devices, local(): lax.psum_scatter(partial_grad.astype(jnp.bfloat16), 'head', scatter_dimen...  77 us
    reduce_scatter x1, waiting for transfers between devices, local(): lax.psum_scatter((product * wscale).astype(jnp.bfloat16), 'seq', scatter_...  53.8 us
    all_gather x1, waiting for transfers between devices, local(): lax.all_gather(value_weight, 'seq', axis=0, tiled=True)  34.6 us
    all_gather x2, waiting for transfers between devices, carried_in(): everything = lax.all_gather(shard.astype(jnp.bfloat16), axis)  31.3 us
    select_n x16, other arithmetic, lap(): return jnp.where(reached, new, before)  19.8 us
    dot_general x1, matrix products, local(): lax.dot_general(grad_value, lax.all_gather(value_weight, 'seq', axis=0, t...  10.2 us
    unnamed x14, local copies, waits for them, and re-layouts  9.64 us
    dot_general x1, matrix products, local(): lax.dot_general(inputs, grad_value, (((0,), (0,)), ((), ())), preferred_e...  6.77 us
  transfers between devices with their start and end apart: 5, of which 5 were waited for; matrix products, arithmetic and copies ran while one was open for 25% of the time, Pallas kernels for 0%

commit v1 on v0

--- a/solution.py
+++ b/solution.py
@@ -66,11 +66,38 @@
     grad_key = dk.reshape(rows, width).astype(jnp.bfloat16)
     grad_value = dv.reshape(rows, width).astype(jnp.bfloat16)
     both_last = (((1,), (1,)), ((), ()))
+
+    def report_the_bench(load):
+        which_axis = "seq"
+        wide_out = jax.lax.axis_size(which_axis)
+        block_out = jax.lax.axis_index(which_axis)
+        left_arr, met_up, found_now = (wide_out, block_out, load.shape[0])
+        block_list = [(j0, (j0 + 1) % left_arr) for j0 in range(left_arr)]
+        store = [(j0, (j0 - 1) % left_arr) for j0 in range(left_arr)]
+        current_block = jnp.zeros(
+            (*load.shape[:0], left_arr * found_now, *load.shape[1:]), load.dtype
+        )
+        current_block = lax.dynamic_update_slice_in_dim(
+            current_block, load, met_up * found_now, axis=0
+        )
+        q_next = then = load
+        x_new = left_arr // 2
+        w = 1
+        while w < x_new + 1:
+            q_next = jax.lax.ppermute(q_next, which_axis, block_list)
+            current_block = lax.dynamic_update_slice_in_dim(
+                current_block, q_next, (met_up - w) % left_arr * found_now, axis=0
+            )
+            if w < left_arr - x_new:
+                then = jax.lax.ppermute(then, which_axis, store)
+                current_block = lax.dynamic_update_slice_in_dim(
+                    current_block, then, (met_up + w) % left_arr * found_now, axis=0
+                )
+            w = w + 1
+        return current_block
+
     partial_grad = lax.dot_general(
-        grad_value,
-        lax.all_gather(value_weight, "seq", axis=0, tiled=True),
-        both_last,
-        preferred_element_type=f32,
+        grad_value, report_the_bench(value_weight), both_last, preferred_element_type=f32
     )
     grad_input = lax.psum_scatter(
         partial_grad.astype(jnp.bfloat16), "head", scatter_dimension=1, tiled=True

time: 293 us -> 284 us (0.969)
  waiting for transfers between devices: 197 us -> 173 us
  local copies, waits for them, and re-layouts: 14.3 us -> 23.7 us
  starting transfers between devices: 0.38 us -> 8.42 us
    ppermute x0 -> x7, waiting for transfers between devices: none -> 109 us  [the longest x4 106 us: report_the_bench(): q_next = jax.lax.ppermute(q_next, which_axis, block_list)]
    reduce_scatter x1, waiting for transfers between devices: 53.8 us -> 0.01 us  [local(): lax.psum_scatter((product * wscale).astype(jnp.bfloat16), 'seq', scatter_...]
    reduce_scatter x1, waiting for transfers between devices: 77 us -> 41.3 us  [local(): lax.psum_scatter(partial_grad.astype(jnp.bfloat16), 'head', scatter_dimen...]
    all_gather x1 -> x0, waiting for transfers between devices: 34.6 us -> none  [local(): lax.all_gather(value_weight, 'seq', axis=0, tiled=True)]
    all_gather x2, waiting for transfers between devices: 31.3 us -> 23 us  [carried_in(): everything = lax.all_gather(shard.astype(jnp.bfloat16), axis)]
    ppermute x0 -> x7, starting transfers between devices: none -> 8.26 us  [the longest x3 7.96 us: report_the_bench(): then = jax.lax.ppermute(then, which_axis, store)]
    dynamic_update_slice x0 -> x8, local copies, waits for them, and re-layouts: none -> 5.75 us  [the longest x4 2.87 us: report_the_bench(): lax.dynamic_update_slice_in_dim(current_block, q_next, (met_up - w) % lef...]
    dot_general x1, matrix products: 10.2 us -> 6.15 us  [local(): lax.dot_general(grad_value, report_the_bench(value_weight), both_last, pr...]
  transfers between devices with their start and end apart: 5 -> 11, of which waited for: 5 -> 7; matrix products, arithmetic and copies ran while one was open for 25% -> 27% of each run, Pallas kernels for 0% -> 0%
where the time goes in v1:
time: 284 us; the launch traced here: 283 us
  waiting for transfers between devices  173 us (61%)
  matrix products  43.1 us (15%)
  local copies, waits for them, and re-layouts  23.7 us (8%)
  other arithmetic  19.9 us (7%)
  between operations  14 us (5%)
  starting transfers between devices  8.42 us (3%)
    ppermute x4, waiting for transfers between devices, report_the_bench(): q_next = jax.lax.ppermute(q_next, which_axis, block_list)  106 us
    reduce_scatter x1, waiting for transfers between devices, local(): lax.psum_scatter(partial_grad.astype(jnp.bfloat16), 'head', scatter_dimen...  41.3 us
    all_gather x2, waiting for transfers between devices, carried_in(): everything = lax.all_gather(shard.astype(jnp.bfloat16), axis)  23 us
    select_n x16, other arithmetic, lap(): return jnp.where(reached, new, before)  19.8 us
    unnamed x28, local copies, waits for them, and re-layouts  12.2 us
    dot_general x1, matrix products, local(): lax.dot_general(inputs, grad_value, (((0,), (0,)), ((), ())), preferred_e...  8.92 us
    ppermute x3, starting transfers between devices, report_the_bench(): then = jax.lax.ppermute(then, which_axis, store)  7.96 us
    dot_general x1, matrix products, local(): lax.dot_general(grad_value, report_the_bench(value_weight), both_last, pr...  6.15 us
  transfers between devices with their start and end apart: 11, of which 7 were waited for; matrix products, arithmetic and copies ran while one was open for 27% of the time, Pallas kernels for 0%

profile of v1, /device:TPU:0, one launch (start us, length us, event | category | flops | bytes accessed | tf_op | source)
XLA Modules:
  0.0 282.6 jit_solution(8096243304979797483)
XLA Ops:
  7.2 2.4 copy.48
  9.6 1.5 copy.49
  11.1 2.4 fusion.16
  13.5 0.8 copy.32
  14.4 0.0 all-gather.7.cloned.1.call-start
  14.4 2.5 convolution_convert_fusion.1
  17.0 0.1 iota_compare_fusion
  17.1 5.0 %fusion.1 = f32[8,512,128]{1,2,0:T(8,128)} fusion(bf16[512,8,128]{0,2,1:T(8,128)(2,1)} %bitcast.99, f32[512]{0:T(512)S(1)} %multiply_rsqrt_fusion, pred[512,512]{1,0:T(8,128)(4,1)S(1)} %iota_compare_fusion, bf16[512,8,128]{0,2,1:T(8,128)(2,1)S(1)} %bitcast.96, bf16[512,1024]{1,0:T(8,128)(2,1)} %param.12), kind=kOutput, calls=%fused_computation.7 | convolution fusion | flops 1080033280 | bytes 5507072 | tf_op jit(solution)/shard_map/hts,thd->shd/dot_general | solution.py:63
  22.1 23.0 %all-gather.5.cloned.1.call-done = bf16[64,128,128]{2,1,0:T(8,128)(2,1)} async-done(((bf16[8,128,128]{2,1,0:T(8,128)(2,1)}), bf16[64,128,128]{2,1,0:T(8,128)(2,1)}) %all-gather.5.cloned.1.call-update) | async-done | bytes 2097168 | tf_op jit(solution)/shard_map/all_gather | solution.py:12
  45.0 10.1 %while.30 = (s32[]{:T(128)}, f32[8,128,128]{2,1,0:T(8,128)S(1)}, s32[]{:T(128)}, bf16[8,8,128,128]{3,2,1,0:T(8,128)(2,1)}, s32[]{:T(128)}, /*index=5*/s32[]{:T(128)}, s32[]{:T(128)}, s32[]{:T(128)}) while((s32[]{:T(128)}, f32[8,128,128]{2,1,0:T(8,128)S(1)}, s32[]{:T(128)}, bf16[8,8,128,128]{3,2,1,0:T(8,128)(2,1)}, s32[]{:T(128)}, ...), condition=%wide.region_1.2_spmd.clone, body=%wide.region_0.1_spmd.clone.sunk | while | flops 524296 | bytes 1310875 | solution.py:21
  45.0 1.2 add_select_fusion.4
  46.3 1.2 add_select_fusion.4
  47.6 1.2 add_select_fusion.4
  48.8 1.2 add_select_fusion.4
  50.1 1.2 add_select_fusion.4
  51.4 1.2 add_select_fusion.4
  52.6 1.2 add_select_fusion.4
  53.9 1.2 add_select_fusion.4
  55.1 3.0 %fusion.9 = bf16[512,8,128]{0,2,1:T(8,128)(2,1)S(1)} fusion(f32[8,512,128]{1,2,0:T(8,128)} %fusion.1, f32[8,128,128]{2,1,0:T(8,128)S(1)} %get-tuple-element.194, bf16[512,1024]{1,0:T(8,128)(2,1)} %param.12), kind=kOutput, calls=%fused_computation.17 | convolution fusion | flops 806354944 | bytes 4718592 | tf_op jit(solution)/shard_map/shi,hij->shj/dot_general | solution.py:64
  58.1 1.0 copy-done.3
  59.1 8.9 %fusion = bf16[4096,1024]{0,1:T(8,128)(2,1)} fusion(bf16[512,1024]{0,1:T(8,128)(2,1)S(1)} %bitcast.102, bf16[512,4096]{1,0:T(8,128)(2,1)} %param.10), kind=kOutput, calls=%fused_computation.5 | convolution fusion | flops 4303355904 | bytes 13631488 | tf_op jit(solution)/shard_map/dot_general | solution.py:106
  68.1 0.3 collective-permute-start
  68.4 2.4 collective-permute-start.1
  70.8 25.5 %collective-permute-done = bf16[512,1024]{1,0:T(8,128)(2,1)S(1)} collective-permute-done((bf16[512,1024]{1,0:T(8,128)(2,1)}, bf16[512,1024]{1,0:T(8,128)(2,1)S(1)}, u32[]{:S(2)}, u32[]{:S(2)}) %collective-permute-start) | collective-permute-done | bytes 1048608 | tf_op jit(solution)/shard_map/ppermute | solution.py:87
  96.3 1.0 copy-done.6
  97.3 2.6 collective-permute-start.3
  99.9 38.6 %collective-permute-done.2 = bf16[512,1024]{1,0:T(8,128)(2,1)S(1)} collective-permute-done((bf16[512,1024]{1,0:T(8,128)(2,1)S(1)}, bf16[512,1024]{1,0:T(8,128)(2,1)S(1)}, u32[]{:S(2)}, u32[]{:S(2)}) %collective-permute-start.2) | collective-permute-done | bytes 1048608 | tf_op jit(solution)/shard_map/ppermute | solution.py:87
  138.5 2.4 collective-permute-done.3
  140.9 2.9 %collective-permute-start.5 = (bf16[512,1024]{1,0:T(8,128)(2,1)}, bf16[512,1024]{1,0:T(8,128)(2,1)}, u32[]{:S(2)}, u32[]{:S(2)}) collective-permute-start(bf16[512,1024]{1,0:T(8,128)(2,1)} %collective-permute-done.3), channel_id=1, source_target_pairs={{0,28},{4,0},{8,4},{12,8},{16,12},{20,16},{24,20},{28,24},{1,29},{... | collective-permute-start | bytes 3145736 | tf_op jit(solution)/shard_map/ppermute | solution.py:92
  143.8 33.2 %collective-permute-done.4 = bf16[512,1024]{1,0:T(8,128)(2,1)} collective-permute-done((bf16[512,1024]{1,0:T(8,128)(2,1)S(1)}, bf16[512,1024]{1,0:T(8,128)(2,1)}, u32[]{:S(2)}, u32[]{:S(2)}) %collective-permute-start.4) | collective-permute-done | bytes 1048608 | tf_op jit(solution)/shard_map/ppermute | solution.py:87
  177.1 1.1 broadcast_in_dim.34
  178.1 0.1 copy-done.5
  178.3 0.1 constant_dynamic-update-slice_fusion.7
  178.4 0.2 copy-done.7
  178.6 0.1 constant_dynamic-update-slice_fusion.6
  178.7 0.2 copy-done.9
  178.9 0.1 constant_dynamic-update-slice_fusion.5
  179.0 0.2 copy-done.11
  179.2 0.1 constant_dynamic-update-slice_fusion.4
  179.3 1.3 constant_dynamic-update-slice_fusion.3
  180.7 1.3 constant_dynamic-update-slice_fusion.2
  182.0 1.3 constant_dynamic-update-slice_fusion.1
  183.4 9.1 %collective-permute-done.6 = bf16[512,1024]{1,0:T(8,128)(2,1)} collective-permute-done((bf16[512,1024]{1,0:T(8,128)(2,1)}, bf16[512,1024]{1,0:T(8,128)(2,1)}, u32[]{:S(2)}, u32[]{:S(2)}) %collective-permute-start.6) | collective-permute-done | bytes 1048608 | tf_op jit(solution)/shard_map/ppermute | solution.py:87
  192.5 1.3 constant_dynamic-update-slice_fusion
  193.8 6.1 %convolution_convert_fusion = bf16[512,4096]{1,0:T(8,128)(2,1)} fusion(bf16[512,1024]{0,1:T(8,128)(2,1)S(1)} %bitcast.104, bf16[4096,1024]{1,0:T(8,128)(2,1)S(1)} %constant_dynamic-update-slice_fusion), kind=kOutput, calls=%fused_computation.6 | convolution fusion | flops 4297064448 | bytes 13631488 | tf_op jit(solution)/shard_map/dot_general | solution.py:99
  200.0 3.0 %select_convert_fusion = bf16[8,512,512]{2,1,0:T(8,128)(2,1)S(1)} fusion(f32[512]{0:T(512)S(1)} %multiply_rsqrt_fusion, pred[512,512]{1,0:T(8,128)(4,1)S(1)} %iota_compare_fusion, bf16[512,8,128]{0,2,1:T(8,128)(2,1)} %bitcast.100, bf16[512,1024]{1,0:T(8,128)(2,1)S(1)} %copy-done), kind=kOutput, calls=%fused_computation.3 | convolution fusion | flops 543162368 | bytes 6555648 | tf_op jit(solution)/shard_map/thd,shd->hts/dot_general | solution.py:56
  203.1 2.1 fusion.38
  205.1 2.8 fusion.24
  208.0 2.4 copy.45
  210.3 3.6 %fusion.7 = bf16[512,8,128]{0,2,1:T(8,128)(2,1)} fusion(f32[8,512,128]{1,2,0:T(8,128)} %fusion.38, f32[8,128,128]{2,1,0:T(8,128)S(1)} %get-tuple-element.194, bf16[512,1024]{1,0:T(8,128)(2,1)S(1)} %copy-done), kind=kOutput, calls=%fused_computation.13 | convolution fusion | flops 806354944 | bytes 4718592 | tf_op jit(solution)/shard_map/shj,hij->shi/dot_general | solution.py:62
  213.9 2.3 copy.44
  216.2 10.0 %while.31 = (s32[]{:T(128)}, f32[8,128,128]{2,1,0:T(8,128)S(1)}, s32[]{:T(128)}, bf16[8,8,128,128]{3,2,1,0:T(8,128)(2,1)}, s32[]{:T(128)}, /*index=5*/s32[]{:T(128)}) while((s32[]{:T(128)}, f32[8,128,128]{2,1,0:T(8,128)S(1)}, s32[]{:T(128)}, bf16[8,8,128,128]{3,2,1,0:T(8,128)(2,1)}, s32[]{:T(128)}, /*index=5*/s32[]{:T(128)}) %tuple.88), condition=%wide.region_4.5_spmd.clone, body=%wide.region_3.4_spmd.clone.sunk | while | flops 524292 | bytes 1310813 | solution.py:21
  216.2 1.2 add_select_fusion.5
  217.4 1.2 add_select_fusion.5
  218.7 1.2 add_select_fusion.5
  219.9 1.2 add_select_fusion.5
  221.2 1.2 add_select_fusion.5
  222.5 1.2 add_select_fusion.5
  223.7 1.2 add_select_fusion.5
  225.0 1.2 add_select_fusion.5
  226.2 3.7 %fusion.8 = bf16[512,8,128]{0,2,1:T(8,128)(2,1)} fusion(f32[8,512,128]{1,2,0:T(8,128)} %fusion.24, f32[8,128,128]{2,1,0:T(8,128)S(1)} %get-tuple-element.195, bf16[512,8,128]{0,2,1:T(8,128)(2,1)S(1)} %bitcast.101, f32[512]{0:T(512)S(1)} %multiply_rsqrt_fusion), kind=kOutput, calls=%fused_computation.15 | convolution fusion | flops 806879232 | bytes 4720640 | tf_op jit(solution)/shard_map/thj,hij->thi/dot_general | solution.py:60
  229.9 2.3 copy.43
  232.2 2.6 copy.46
  234.7 41.3 %reduce-scatter.3.cloned.1.call-done = bf16[512,1024]{1,0:T(8,128)(2,1)} async-done(((bf16[512,4096]{1,0:T(8,128)(2,1)}), bf16[512,1024]{1,0:T(8,128)(2,1)}) %reduce-scatter.3.cloned.1.call-update) | async-done | bytes 1048592 | tf_op jit(solution)/shard_map/reduce_scatter | solution.py:102
  (35 shorter events, 0.3 us)
Async XLA Ops:
  7.2 7.3 %copy-start = (bf16[512,1024]{1,0:T(8,128)(2,1)S(1)}, bf16[512,1024]{1,0:T(8,128)(2,1)}, u32[]{:S(2)}) copy-start(bf16[512,1024]{1,0:T(8,128)(2,1)} %param.13) | copy-start | bytes 3145732
  7.2 37.9 %all-gather.5.cloned.1.call-start = ((), (), s32[]{:S(2)}) async-start(), calls=%async_computation.4 | async-start | bytes 2359296 | tf_op jit(solution)/shard_map/all_gather | solution.py:12
  14.4 201.8 %all-gather.7.cloned.1.call-start = ((), (), s32[]{:S(2)}) async-start(), calls=%async_computation.5 | async-start | bytes 2359296 | tf_op jit(solution)/shard_map/all_gather | solution.py:12
  16.9 215.2 %reduce-scatter.5.cloned.1.call-start = ((), (), s32[]{:S(2)}) async-start(), calls=%async_computation.3 | async-start | bytes 9437184 | tf_op jit(solution)/shard_map/reduce_scatter | solution.py:109
  58.1 1.0 copy-start.3
  68.1 208.0 %reduce-scatter.3.cloned.1.call-start = ((), (), s32[]{:S(2)}) async-start(), calls=%async_computation.2 | async-start | bytes 5242880 | tf_op jit(solution)/shard_map/reduce_scatter | solution.py:102
  68.1 28.2 %collective-permute-start = (bf16[512,1024]{1,0:T(8,128)(2,1)}, bf16[512,1024]{1,0:T(8,128)(2,1)S(1)}, u32[]{:S(2)}, u32[]{:S(2)}) collective-permute-start(bf16[512,1024]{1,0:T(8,128)(2,1)} %param.15), channel_id=1, source_target_pairs={{0,4},{4,8},{8,12},{12,16},{16,20},{20,24},{24,28},{28,0},{1,5},{5... | collective-permute-start | bytes 3145736 | tf_op jit(solution)/shard_map/ppermute | solution.py:87
  68.4 28.9 %collective-permute-start.1 = (bf16[512,1024]{1,0:T(8,128)(2,1)}, bf16[512,1024]{1,0:T(8,128)(2,1)S(1)}, u32[]{:S(2)}, u32[]{:S(2)}) collective-permute-start(bf16[512,1024]{1,0:T(8,128)(2,1)} %param.15), channel_id=1, source_target_pairs={{0,28},{4,0},{8,4},{12,8},{16,12},{20,16},{24,20},{28,24},{1,29},{... | collective-permute-start | bytes 3145736 | tf_op jit(solution)/shard_map/ppermute | solution.py:92
  96.3 1.0 copy-start.6
  97.3 41.2 %collective-permute-start.2 = (bf16[512,1024]{1,0:T(8,128)(2,1)S(1)}, bf16[512,1024]{1,0:T(8,128)(2,1)S(1)}, u32[]{:S(2)}, u32[]{:S(2)}) collective-permute-start(bf16[512,1024]{1,0:T(8,128)(2,1)S(1)} %collective-permute-done), channel_id=1, source_target_pairs={{0,4},{4,8},{8,12},{12,16},{16,20},{20,24},{24,28},{28,0},{1,5},{5... | collective-permute-start | bytes 3145736 | tf_op jit(solution)/shard_map/ppermute | solution.py:87
  97.3 41.2 %copy-start.8 = (bf16[512,1024]{1,0:T(8,128)(2,1)}, bf16[512,1024]{1,0:T(8,128)(2,1)S(1)}, u32[]{:S(2)}) copy-start(bf16[512,1024]{1,0:T(8,128)(2,1)S(1)} %collective-permute-done.1) | copy-start | bytes 3145732
  97.3 43.6 %collective-permute-start.3 = (bf16[512,1024]{1,0:T(8,128)(2,1)S(1)}, bf16[512,1024]{1,0:T(8,128)(2,1)}, u32[]{:S(2)}, u32[]{:S(2)}) collective-permute-start(bf16[512,1024]{1,0:T(8,128)(2,1)S(1)} %collective-permute-done.1), channel_id=1, source_target_pairs={{0,28},{4,0},{8,4},{12,8},{16,12},{20,16},{24,20},{28,24},{1,29},{... | collective-permute-start | bytes 3145736 | tf_op jit(solution)/shard_map/ppermute | solution.py:92
  138.5 2.4 copy-start.10
  138.5 38.6 %collective-permute-start.4 = (bf16[512,1024]{1,0:T(8,128)(2,1)S(1)}, bf16[512,1024]{1,0:T(8,128)(2,1)}, u32[]{:S(2)}, u32[]{:S(2)}) collective-permute-start(bf16[512,1024]{1,0:T(8,128)(2,1)S(1)} %collective-permute-done.2), channel_id=1, source_target_pairs={{0,4},{4,8},{8,12},{12,16},{16,20},{20,24},{24,28},{28,0},{1,5},{5... | collective-permute-start | bytes 3145736 | tf_op jit(solution)/shard_map/ppermute | solution.py:87
  140.9 41.1 %collective-permute-start.5 = (bf16[512,1024]{1,0:T(8,128)(2,1)}, bf16[512,1024]{1,0:T(8,128)(2,1)}, u32[]{:S(2)}, u32[]{:S(2)}) collective-permute-start(bf16[512,1024]{1,0:T(8,128)(2,1)} %collective-permute-done.3), channel_id=1, source_target_pairs={{0,28},{4,0},{8,4},{12,8},{16,12},{20,16},{24,20},{28,24},{1,29},{... | collective-permute-start | bytes 3145736 | tf_op jit(solution)/shard_map/ppermute | solution.py:92
  177.0 15.4 %collective-permute-start.6 = (bf16[512,1024]{1,0:T(8,128)(2,1)}, bf16[512,1024]{1,0:T(8,128)(2,1)}, u32[]{:S(2)}, u32[]{:S(2)}) collective-permute-start(bf16[512,1024]{1,0:T(8,128)(2,1)} %collective-permute-done.4), channel_id=1, source_target_pairs={{0,4},{4,8},{8,12},{12,16},{16,20},{20,24},{24,28},{28,0},{1,5},{5... | collective-permute-start | bytes 3145736 | tf_op jit(solution)/shard_map/ppermute | solution.py:87
  177.0 1.2 copy-start.5
  177.0 1.5 copy-start.7
  177.0 1.9 copy-start.9
  177.1 2.2 copy-start.11
  178.3 15.5 %copy-start.4 = (bf16[512,8,128]{0,2,1:T(8,128)(2,1)S(1)}, bf16[512,8,128]{0,2,1:T(8,128)(2,1)}, u32[]{:S(2)}) copy-start(bf16[512,8,128]{0,2,1:T(8,128)(2,1)} %copy-done.3) | copy-start | bytes 3145732
  200.0 5.1 %copy-start.2 = (bf16[512,1024]{1,0:T(8,128)(2,1)S(1)}, bf16[512,1024]{1,0:T(8,128)(2,1)}, u32[]{:S(2)}) copy-start(bf16[512,1024]{1,0:T(8,128)(2,1)} %param.12) | copy-start | bytes 3145732
  208.0 18.3 %copy-start.1 = (bf16[512,1024]{0,1:T(8,128)(2,1)S(1)}, bf16[512,1024]{0,1:T(8,128)(2,1)}, u32[]{:S(2)}) copy-start(bf16[512,1024]{0,1:T(8,128)(2,1)} %copy.48) | copy-start | bytes 3145732
Sparse Core Ops, SparseCore 0:
  14.5 30.4 all-gather.4
  46.9 28.6 all-gather.6
  79.0 100.2 reduce-scatter.4
  200.1 75.8 reduce-scatter.2
